TPU v7x, 32 devices: a whole 2x2x4 slice. The times are simulated.
32 devices in a mesh: dp: 8 (over y, x, core), mp: 4 (over z).
Axes of the slice: x: 2, y: 2, z: 4, core: 2. Of those that a mesh axis runs over, the one named last changes fastest.
Arguments:
- hidden_in: bfloat16 [2, 8192, 2048], P(None, ('dp', 'mp')), may hold values from -6 to 6
- counts: int32 [2, 8], P(None, 'dp'), may hold values from 20 to 50, as said below
- summary: float32 [50, 2048], replicated, may hold values from -6 to 6
- query_weight: bfloat16 [2048, 2048], P('dp', 'mp'), may hold values from -0.125 to 0.125
- query_bias: bfloat16 [2048], P('mp'), may hold values from -1.75 to 1.75
- key_weight: bfloat16 [2048, 2048], P('dp', 'mp'), may hold values from -0.125 to 0.125
- value_weight: bfloat16 [2048, 2048], P('dp', 'mp'), may hold values from -0.125 to 0.125
- value_bias: bfloat16 [2048], P('mp'), may hold values from -1.75 to 1.75
- out_weight: bfloat16 [2048, 2048], P('mp', 'dp'), may hold values from -2 to 2
- out_bias: bfloat16 [2048], replicated, may hold values from -1.25 to 1.25
- up_weight: bfloat16 [2048, 8192], P('dp', 'mp'), may hold values from -0.125 to 0.125
- up_bias: bfloat16 [8192], P('mp'), may hold values from -1.75 to 1.75
- down_weight: bfloat16 [8192, 2048], P('mp', 'dp'), may hold values from -0.0625 to 0.0625
- down_bias: bfloat16 [2048], replicated, may hold values from -1.25 to 1.25
- attn_gain: float32 [2048], replicated, may hold values from 0.5 to 1.5
- attn_shift: float32 [2048], replicated, may hold values from -0.625 to 0.625
- mlp_gain: float32 [2048], replicated, may hold values from 0.5 to 1.5
- mlp_shift: float32 [2048], replicated, may hold values from -0.625 to 0.625
- cotangent: bfloat16 [2, 8192, 2048], P(None, ('dp', 'mp')), may hold values from -6 to 6
Outputs:
- layer_out: bfloat16 [2, 8192, 2048], P(None, ('dp', 'mp'))
- grad_input: float32 [2, 8192, 2048], P(None, ('dp', 'mp'))
- grad_summary: float32 [50, 2048], replicated
- grad_query_weight: float32 [2048, 2048], P('dp', 'mp')
- grad_query_bias: float32 [2048], P('mp')
- grad_key_weight: float32 [2048, 2048], P('dp', 'mp')
- grad_value_weight: float32 [2048, 2048], P('dp', 'mp')
- grad_value_bias: float32 [2048], P('mp')
- grad_out_weight: float32 [2048, 2048], P('mp', 'dp')
- grad_out_bias: float32 [2048], replicated
- grad_up_weight: float32 [2048, 8192], P('dp', 'mp')
- grad_up_bias: float32 [8192], P('mp')
- grad_down_weight: float32 [8192, 2048], P('mp', 'dp')
- grad_down_bias: float32 [2048], replicated
- grad_attn_gain: float32 [2048], replicated
- grad_attn_shift: float32 [2048], replicated
- grad_mlp_gain: float32 [2048], replicated
- grad_mlp_shift: float32 [2048], replicated
Inputs may be any that keep to these rules, and one draw needn't show every extreme that they name: `counts`: an item's count c marks the first c of its 50 prefix slots and the first c of its 50 appended slots as used.
All inputs are finite; a program needn't handle non-finite values.
Results may differ from a plain program's by a relative error of at most 0.02.
Values may be sent and summed in bfloat16 or wider, within the bound.
No kernel may reach another device: no remote copies, remote signals or barrier semaphores. Data moves between devices by JAX's collectives and lax.ppermute only.
A program may use at most 256 MiB of HBM per device.

v0:
```python
import math
import jax
import jax.numpy as jnp
from jax import lax
from jax.sharding import PartitionSpec as P

D = 2048
HD = 64
SUMM = 50
precise = lax.Precision.HIGHEST
gelu_coef = math.sqrt(2.0 / math.pi)


def gelu_slope(values_in):
    inner = gelu_coef * (values_in + 0.044715 * values_in * values_in * values_in)
    tangent = jnp.tanh(inner)
    return 0.5 * (1.0 + tangent) + 0.5 * values_in * (1.0 - tangent * tangent) * gelu_coef * (
        1.0 + 3.0 * 0.044715 * values_in * values_in
    )


def layer_norm(values_in, gain_vec, shift_vec):
    centred = values_in - jnp.mean(values_in, axis=-1, keepdims=True)
    spread = jnp.mean(centred * centred, axis=-1, keepdims=True)
    scaled = lax.rsqrt(spread + 1e-05)
    unit_rows = centred * scaled
    return (unit_rows * gain_vec + shift_vec, unit_rows, scaled)


def norm_back(grad_out, unit_rows, scaled, gain_vec):
    weighted = grad_out * gain_vec
    return scaled * (
        weighted
        - jnp.mean(weighted, axis=-1, keepdims=True)
        - unit_rows * jnp.mean(weighted * unit_rows, axis=-1, keepdims=True)
    )


def dense(left_side, right_side):
    return jnp.dot(left_side, right_side, preferred_element_type=jnp.float32)


def times_t(left_side, right_side):
    return lax.dot_general(
        left_side, right_side, (((1,), (1,)), ((), ())), preferred_element_type=jnp.float32
    )


def inner_rows(left_side, right_side):
    return lax.dot_general(
        left_side, right_side, (((0,), (0,)), ((), ())), preferred_element_type=jnp.float32
    )


def live_keys(seq_len, item_count):
    positions = jnp.arange(seq_len, dtype=jnp.int32)
    slot_ids = positions - (seq_len - SUMM)
    return (
        (positions >= SUMM) & (slot_ids < 0)
        | (positions < item_count)
        | (slot_ids >= 0) & (slot_ids < item_count)
    )


def block_mask(row_begin, block_rows, key_live):
    rows_here = row_begin + jnp.arange(block_rows, dtype=jnp.int32)
    columns = jnp.arange(key_live.shape[0], dtype=jnp.int32)
    return (columns[None, :] <= rows_here[:, None]) & key_live[None, :]


def shards(
    hidden_in,
    counts,
    summary,
    query_weight,
    query_bias,
    key_weight,
    value_weight,
    value_bias,
    out_weight,
    out_bias,
    up_weight,
    up_bias,
    down_weight,
    down_bias,
    attn_gain,
    attn_shift,
    mlp_gain,
    mlp_shift,
    cotangent,
):
    micro_total = hidden_in.shape[0]
    local_rows = hidden_in.shape[1]
    seq_len = local_rows * lax.axis_size("mp")
    row_offset = lax.axis_index("mp") * local_rows
    head_cols = query_weight.shape[1]
    ff_cols = up_weight.shape[1]
    local_heads = head_cols // HD
    block_rows = 512
    block_count = seq_len // block_rows
    qk_scale = HD ** (-0.5)
    bias_query = query_bias.astype(jnp.float32)
    bias_value = value_bias.astype(jnp.float32)
    bias_up = up_bias.astype(jnp.float32)
    bias_out = out_bias.astype(jnp.float32)
    bias_down = down_bias.astype(jnp.float32)
    positions = row_offset + jnp.arange(local_rows, dtype=jnp.int32)
    picker = (
        (positions - (seq_len - SUMM))[:, None] == jnp.arange(SUMM, dtype=jnp.int32)[None, :]
    ).astype(jnp.float32)
    summary_rows = jnp.dot(picker, summary, precision=precise)
    full_shapes = (
        (D, head_cols),
        (D, head_cols),
        (D, head_cols),
        (head_cols, D),
        (D, ff_cols),
        (ff_cols, D),
    )
    full_sums = tuple((jnp.zeros(shape_pair, jnp.float32) for shape_pair in full_shapes))
    head_sums = (
        jnp.zeros((head_cols,), jnp.float32),
        jnp.zeros((head_cols,), jnp.float32),
        jnp.zeros((ff_cols,), jnp.float32),
    )
    zero_width = jnp.zeros((D,), jnp.float32)
    row_sums = (
        zero_width,
        zero_width,
        zero_width,
        zero_width,
        zero_width,
        zero_width,
        jnp.zeros((SUMM, D), jnp.float32),
    )
    outputs = []
    input_grads = []
    for micro_step in range(micro_total):
        gathered = (
            lax.all_gather(query_weight, "dp", axis=0, tiled=True),
            lax.all_gather(key_weight, "dp", axis=0, tiled=True),
            lax.all_gather(value_weight, "dp", axis=0, tiled=True),
            lax.all_gather(out_weight, "dp", axis=1, tiled=True),
            lax.all_gather(up_weight, "dp", axis=0, tiled=True),
            lax.all_gather(down_weight, "dp", axis=1, tiled=True),
        )
        query_full, key_full, value_full, out_full, up_full, down_full = gathered
        key_live = live_keys(seq_len, counts[micro_step, 0])
        joined = hidden_in[micro_step].astype(jnp.float32) + summary_rows
        normed, unit_one, scale_one = layer_norm(joined, attn_gain, attn_shift)
        shard_rows = lax.all_gather(normed.astype(jnp.bfloat16), "mp", axis=0, tiled=True)
        query_part = ((dense(shard_rows, query_full) + bias_query) * qk_scale).astype(jnp.bfloat16)
        key_part = dense(shard_rows, key_full).astype(jnp.bfloat16)
        value_part = (dense(shard_rows, value_full) + bias_value).astype(jnp.bfloat16)
        projected = jnp.concatenate((shard_rows, query_part, key_part, value_part), axis=1)
        normed_full = projected[:, :D]
        query_rows = projected[:, D : D + head_cols].reshape(seq_len, local_heads, HD)
        key_rows = projected[:, D + head_cols : D + 2 * head_cols].reshape(seq_len, local_heads, HD)
        value_rows = projected[:, D + 2 * head_cols :].reshape(seq_len, local_heads, HD)

        def forward_block(block_index):
            row_begin = block_index * block_rows
            query_block = lax.dynamic_slice_in_dim(query_rows, row_begin, block_rows, 0)
            scores = jnp.einsum(
                "qhd,khd->hqk", query_block, key_rows, preferred_element_type=jnp.float32
            )
            scores = jnp.where(block_mask(row_begin, block_rows, key_live)[None], scores, -1e30)
            row_top = jnp.max(scores, axis=-1, keepdims=True)
            exp_scores = jnp.exp(scores - row_top)
            exp_total = jnp.sum(exp_scores, axis=-1, keepdims=True)
            weights_low = (exp_scores / exp_total).astype(jnp.bfloat16)
            block_out = jnp.einsum(
                "hqk,khd->qhd", weights_low, value_rows, preferred_element_type=jnp.float32
            )
            return (
                block_out.astype(jnp.bfloat16).reshape(block_rows, head_cols),
                (row_top + jnp.log(exp_total))[..., 0],
            )

        attn_blocks, log_totals = lax.map(forward_block, jnp.arange(block_count, dtype=jnp.int32))
        attended = attn_blocks.reshape(seq_len, head_cols)
        mixed_rows = (
            joined
            + lax.psum_scatter(
                dense(attended, out_full).astype(jnp.bfloat16),
                "mp",
                scatter_dimension=0,
                tiled=True,
            ).astype(jnp.float32)
            + bias_out
        )
        normed_two, unit_two, scale_two = layer_norm(mixed_rows, mlp_gain, mlp_shift)
        expand_shard_rows = lax.all_gather(
            normed_two.astype(jnp.bfloat16), "mp", axis=0, tiled=True
        )
        up_value = dense(expand_shard_rows, up_full) + bias_up
        expanded = jnp.concatenate(
            (expand_shard_rows, jax.nn.gelu(up_value, approximate=True).astype(jnp.bfloat16)),
            axis=1,
        )
        normed_two_full = expanded[:, :D]
        active = expanded[:, D:]
        layer_rows = (
            mixed_rows
            + lax.psum_scatter(
                dense(active, down_full).astype(jnp.bfloat16), "mp", scatter_dimension=0, tiled=True
            ).astype(jnp.float32)
            + bias_down
        )
        outputs.append(layer_rows.astype(jnp.bfloat16))
        grad_rows = cotangent[micro_step]
        grad_layer = grad_rows.astype(jnp.float32)
        mlp_shard_rows = lax.all_gather(grad_rows, "mp", axis=0, tiled=True)
        mlp_up_value = dense(normed_two_full, up_full) + bias_up
        grad_active = times_t(mlp_shard_rows, down_full)
        mlp_grad_up = (grad_active * gelu_slope(mlp_up_value)).astype(jnp.bfloat16)
        spread_grads = jnp.concatenate((mlp_shard_rows, mlp_grad_up), axis=1)
        grad_full = spread_grads[:, :D]
        grad_up = spread_grads[:, D:]
        micro_down = inner_rows(active, grad_full)
        micro_up = inner_rows(normed_two_full, grad_up)
        up_bias_grad = jnp.sum(grad_up.astype(jnp.float32), axis=0)
        grad_normed_two = lax.psum_scatter(
            times_t(grad_up, up_full).astype(jnp.bfloat16), "mp", scatter_dimension=0, tiled=True
        ).astype(jnp.float32)
        grad_mixed = grad_layer + norm_back(grad_normed_two, unit_two, scale_two, mlp_gain)
        attn_shard_rows = lax.all_gather(grad_mixed.astype(jnp.bfloat16), "mp", axis=0, tiled=True)
        spread_attn = jnp.concatenate(
            (attn_shard_rows, times_t(attn_shard_rows, out_full).astype(jnp.bfloat16)), axis=1
        )
        grad_mixed_full = spread_attn[:, :D]
        grad_attended = spread_attn[:, D:].reshape(seq_len, local_heads, HD)
        micro_out = inner_rows(attended, grad_mixed_full)

        def backward_block(sums_pair, block_index):
            key_sum, value_sum = sums_pair
            row_begin = block_index * block_rows
            query_block = lax.dynamic_slice_in_dim(query_rows, row_begin, block_rows, 0)
            grad_block = lax.dynamic_slice_in_dim(grad_attended, row_begin, block_rows, 0)
            scores = jnp.einsum(
                "qhd,khd->hqk", query_block, key_rows, preferred_element_type=jnp.float32
            )
            scores = jnp.where(block_mask(row_begin, block_rows, key_live)[None], scores, -1e30)
            weights_full = jnp.exp(scores - log_totals[block_index][..., None])
            grad_weights = jnp.einsum(
                "qhd,khd->hqk", grad_block, value_rows, preferred_element_type=jnp.float32
            )
            centre = jnp.sum(weights_full * grad_weights, axis=-1, keepdims=True)
            grad_scores = (weights_full * (grad_weights - centre)).astype(jnp.bfloat16)
            grad_query_block = jnp.einsum(
                "hqk,khd->qhd", grad_scores, key_rows, preferred_element_type=jnp.float32
            )
            key_sum = key_sum + jnp.einsum(
                "hqk,qhd->khd", grad_scores, query_block, preferred_element_type=jnp.float32
            )
            value_sum = value_sum + jnp.einsum(
                "hqk,qhd->khd",
                weights_full.astype(jnp.bfloat16),
                grad_block,
                preferred_element_type=jnp.float32,
            )
            return (
                (key_sum, value_sum),
                grad_query_block.astype(jnp.bfloat16).reshape(block_rows, head_cols),
            )

        zero_heads = jnp.zeros((seq_len, local_heads, HD), jnp.float32)
        (key_sum, value_sum), query_blocks = lax.scan(
            backward_block, (zero_heads, zero_heads), jnp.arange(block_count, dtype=jnp.int32)
        )
        grad_query = query_blocks.reshape(seq_len, head_cols)
        grad_key = key_sum.astype(jnp.bfloat16).reshape(seq_len, head_cols)
        grad_value = value_sum.astype(jnp.bfloat16).reshape(seq_len, head_cols)
        micro_query = inner_rows(normed_full, grad_query) * qk_scale
        micro_key = inner_rows(normed_full, grad_key)
        micro_value = inner_rows(normed_full, grad_value)
        query_bias_grad = jnp.sum(grad_query.astype(jnp.float32), axis=0) * qk_scale
        value_bias_grad = jnp.sum(grad_value.astype(jnp.float32), axis=0)
        grad_normed = lax.psum_scatter(
            (
                times_t(grad_query, query_full) * qk_scale
                + times_t(grad_key, key_full)
                + times_t(grad_value, value_full)
            ).astype(jnp.bfloat16),
            "mp",
            scatter_dimension=0,
            tiled=True,
        ).astype(jnp.float32)
        grad_joined = grad_mixed + norm_back(grad_normed, unit_one, scale_one, attn_gain)
        input_grads.append(grad_joined)
        micro_grads = (micro_query, micro_key, micro_value, micro_out, micro_up, micro_down)
        full_sums = tuple(map(jnp.add, full_sums, micro_grads))
        head_sums = (
            head_sums[0] + query_bias_grad,
            head_sums[1] + value_bias_grad,
            head_sums[2] + up_bias_grad,
        )
        row_sums = (
            row_sums[0] + jnp.sum(grad_mixed, axis=0),
            row_sums[1] + jnp.sum(grad_layer, axis=0),
            row_sums[2] + jnp.sum(grad_normed * unit_one, axis=0),
            row_sums[3] + jnp.sum(grad_normed, axis=0),
            row_sums[4] + jnp.sum(grad_normed_two * unit_two, axis=0),
            row_sums[5] + jnp.sum(grad_normed_two, axis=0),
            row_sums[6] + jnp.dot(picker.T, grad_joined, precision=precise),
        )
    weight_total = (
        lax.psum_scatter(
            full_sums[0].astype(jnp.bfloat16), "dp", scatter_dimension=0, tiled=True
        ).astype(jnp.float32),
        lax.psum_scatter(
            full_sums[1].astype(jnp.bfloat16), "dp", scatter_dimension=0, tiled=True
        ).astype(jnp.float32),
        lax.psum_scatter(
            full_sums[2].astype(jnp.bfloat16), "dp", scatter_dimension=0, tiled=True
        ).astype(jnp.float32),
        lax.psum_scatter(
            full_sums[3].astype(jnp.bfloat16), "dp", scatter_dimension=1, tiled=True
        ).astype(jnp.float32),
        lax.psum_scatter(
            full_sums[4].astype(jnp.bfloat16), "dp", scatter_dimension=0, tiled=True
        ).astype(jnp.float32),
        lax.psum_scatter(
            full_sums[5].astype(jnp.bfloat16), "dp", scatter_dimension=1, tiled=True
        ).astype(jnp.float32),
    )
    head_total = lax.psum((head_sums[0], head_sums[1], head_sums[2]), "dp")
    row_total = lax.psum(
        (row_sums[0], row_sums[1], row_sums[2], row_sums[3], row_sums[4], row_sums[5], row_sums[6]),
        ("dp", "mp"),
    )
    return (
        jnp.stack(outputs),
        jnp.stack(input_grads),
        row_total[6],
        weight_total[0],
        head_total[0],
        weight_total[1],
        weight_total[2],
        head_total[1],
        weight_total[3],
        row_total[0],
        weight_total[4],
        head_total[2],
        weight_total[5],
        row_total[1],
        row_total[2],
        row_total[3],
        row_total[4],
        row_total[5],
    )


def solution(mesh):
    in_specs = (
        P(None, ("dp", "mp"), None),
        P(None, "dp"),
        P(),
        P("dp", "mp"),
        P("mp"),
        P("dp", "mp"),
        P("dp", "mp"),
        P("mp"),
        P("mp", "dp"),
        P(),
        P("dp", "mp"),
        P("mp"),
        P("mp", "dp"),
        P(),
        P(),
        P(),
        P(),
        P(),
        P(None, ("dp", "mp"), None),
    )
    out_specs = (
        P(None, ("dp", "mp"), None),
        P(None, ("dp", "mp"), None),
        P(),
        P("dp", "mp"),
        P("mp"),
        P("dp", "mp"),
        P("dp", "mp"),
        P("mp"),
        P("mp", "dp"),
        P(),
        P("dp", "mp"),
        P("mp"),
        P("mp", "dp"),
        P(),
        P(),
        P(),
        P(),
        P(),
    )
    return jax.shard_map(shards, mesh=mesh, in_specs=in_specs, out_specs=out_specs, check_vma=False)
```

profile of v0, /device:TPU:1, one launch (start us, length us, event | category | flops | bytes accessed | tf_op | source)
XLA Modules:
  0.0 2053.1 jit_solution(16066606750939423374)
XLA Ops:
  17.3 23.1 %all-gather.21.cloned.1.call-done = bf16[2048,512]{1,0:T(8,128)(2,1)} async-done(((bf16[256,512]{1,0:T(8,128)(2,1)}), bf16[2048,512]{1,0:T(8,128)(2,1)}) %all-gather.21.cloned.1.call-update) | async-done | bytes 2097168 | tf_op jit(solution)/shard_map/all_gather | solution.py:141
  40.4 82.5 %all-gather.17.cloned.1.call-done = bf16[1024,2048]{1,0:T(8,128)(2,1)} async-done(((bf16[256,2048]{1,0:T(8,128)(2,1)}), bf16[1024,2048]{1,0:T(8,128)(2,1)}) %all-gather.17.cloned.1.call-update) | async-done | bytes 4194320 | tf_op jit(solution)/shard_map/all_gather | solution.py:151
  128.1 23.5 %all-gather.19.cloned.1.call-done = bf16[2048,512]{1,0:T(8,128)(2,1)} async-done(((bf16[256,512]{1,0:T(8,128)(2,1)}), bf16[2048,512]{1,0:T(8,128)(2,1)}) %all-gather.19.cloned.1.call-update) | async-done | bytes 2097168 | tf_op jit(solution)/shard_map/all_gather | solution.py:140
  156.9 24.4 %all-gather.23.cloned.1.call-done = bf16[2048,512]{1,0:T(8,128)(2,1)} async-done(((bf16[256,512]{1,0:T(8,128)(2,1)}), bf16[2048,512]{1,0:T(8,128)(2,1)}) %all-gather.23.cloned.1.call-update) | async-done | bytes 2097168 | tf_op jit(solution)/shard_map/all_gather | solution.py:142
  188.6 33.1 %while.56 = (s32[]{:T(128)}, bf16[2,512,512]{2,1,0:T(8,128)(2,1)}, f32[2,8,512]{2,1,0:T(8,128)S(1)}, s32[2]{0:T(128)S(1)}, bf16[1024,8,64]{0,2,1:T(8,128)(2,1)S(...) while((s32[]{:T(128)}, bf16[2,512,512]{2,1,0:T(8,128)(2,1)}, ...), condition=%wide.region_5.6_spmd.clone, body=%wide.region_2.5_spmd.clone.sunk | while | flops 1112807936 | bytes 62003432 | solution.py:180
  229.3 64.5 %all-gather.33.cloned.1.call-done = bf16[1024,2048]{1,0:T(8,128)(2,1)} async-done(((bf16[256,2048]{1,0:T(8,128)(2,1)}), bf16[1024,2048]{1,0:T(8,128)(2,1)}) %all-gather.33.cloned.1.call-update) | async-done | bytes 4194320 | tf_op jit(solution)/shard_map/all_gather | solution.py:151
  307.8 33.3 %while.57 = (s32[]{:T(128)}, bf16[2,512,512]{2,1,0:T(8,128)(2,1)}, f32[2,8,512]{2,1,0:T(8,128)S(1)}, s32[2]{0:T(128)S(1)}, bf16[1024,8,64]{0,2,1:T(8,128)(2,1)S(...) while((s32[]{:T(128)}, bf16[2,512,512]{2,1,0:T(8,128)(2,1)}, ...), condition=%wide.region_15.16_spmd.clone, body=%wide.region_12.15_spmd.clone.sunk | while | flops 1112807936 | bytes 62003432 | solution.py:180
  349.1 22.8 %reduce-scatter.15.cloned.1.call-done = bf16[256,2048]{1,0:T(8,128)(2,1)} async-done(((bf16[1024,2048]{1,0:T(8,128)(2,1)}), bf16[256,2048]{1,0:T(8,128)(2,1)}) %reduce-scatter.15.cloned.1.call-update) | async-done | bytes 1048592 | tf_op jit(solution)/shard_map/reduce_scatter | solution.py:184
  371.9 79.7 %reduce-scatter.19.cloned.1.call-done = bf16[256,2048]{1,0:T(8,128)(2,1)} async-done(((bf16[1024,2048]{1,0:T(8,128)(2,1)}), bf16[256,2048]{1,0:T(8,128)(2,1)}) %reduce-scatter.19.cloned.1.call-update) | async-done | bytes 1048592 | tf_op jit(solution)/shard_map/reduce_scatter | solution.py:184
  461.7 47.2 %all-gather.29.cloned.1.call-done = bf16[2048,2048]{1,0:T(8,128)(2,1)} async-done(((bf16[256,2048]{1,0:T(8,128)(2,1)}), bf16[2048,2048]{1,0:T(8,128)(2,1)}) %all-gather.29.cloned.1.call-update) | async-done | bytes 8388624 | tf_op jit(solution)/shard_map/all_gather | solution.py:144
  508.8 82.4 %all-gather.27.cloned.1.call-done = bf16[1024,2048]{1,0:T(8,128)(2,1)} async-done(((bf16[256,2048]{1,0:T(8,128)(2,1)}), bf16[1024,2048]{1,0:T(8,128)(2,1)}) %all-gather.27.cloned.1.call-update) | async-done | bytes 4194320 | tf_op jit(solution)/shard_map/all_gather | solution.py:193
  591.2 14.7 fusion.180
  605.9 66.8 %all-gather.41.cloned.1.call-done = bf16[1,1024,2048]{2,1,0:T(8,128)(2,1)} async-done(((bf16[1,256,2048]{2,1,0:T(8,128)(2,1)}), bf16[1,1024,2048]{2,1,0:T(8,128)(2,1)}) %all-gather.41.cloned.1.call-update) | async-done | bytes 4194320 | tf_op jit(solution)/shard_map/all_gather | solution.py:213
  672.7 56.7 %all-gather.31.cloned.1.call-done = bf16[2048,2048]{1,0:T(8,128)(2,1)} async-done(((bf16[2048,256]{1,0:T(8,128)(2,1)}), bf16[2048,2048]{1,0:T(8,128)(2,1)}) %all-gather.31.cloned.1.call-update) | async-done | bytes 8388624 | tf_op jit(solution)/shard_map/all_gather | solution.py:145
  729.3 18.8 convert_reduce_fusion.1
  750.2 13.0 convolution_convert_fusion.3
  763.2 48.0 %all-gather.35.cloned.1.call-done = bf16[1024,2048]{1,0:T(8,128)(2,1)} async-done(((bf16[256,2048]{1,0:T(8,128)(2,1)}), bf16[1024,2048]{1,0:T(8,128)(2,1)}) %all-gather.35.cloned.1.call-update) | async-done | bytes 4194320 | tf_op jit(solution)/shard_map/all_gather | solution.py:193
  811.3 14.6 fusion.181
  825.8 66.2 %all-gather.43.cloned.1.call-done = bf16[1,1024,2048]{2,1,0:T(8,128)(2,1)} async-done(((bf16[1,256,2048]{2,1,0:T(8,128)(2,1)}), bf16[1,1024,2048]{2,1,0:T(8,128)(2,1)}) %all-gather.43.cloned.1.call-update) | async-done | bytes 4194320 | tf_op jit(solution)/shard_map/all_gather | solution.py:213
  892.0 18.8 convert_reduce_fusion
  912.9 13.4 convolution_convert_fusion.2
  926.3 16.1 convolution_convert_fusion.4
  942.5 16.2 convolution_convert_fusion.6
  959.3 10.8 reduce-scatter.23.cloned.1.call-done
  970.1 79.5 %reduce-scatter.27.cloned.1.call-done = bf16[256,2048]{1,0:T(8,128)(2,1)} async-done(((bf16[1024,2048]{1,0:T(8,128)(2,1)}), bf16[256,2048]{1,0:T(8,128)(2,1)}) %reduce-scatter.27.cloned.1.call-update) | async-done | bytes 1048592 | tf_op jit(solution)/shard_map/reduce_scatter | solution.py:223
  1053.8 75.2 %reduce-scatter.21.cloned.1.call-done = bf16[256,2048]{1,0:T(8,128)(2,1)} async-done(((bf16[1024,2048]{1,0:T(8,128)(2,1)}), bf16[256,2048]{1,0:T(8,128)(2,1)}) %reduce-scatter.21.cloned.1.call-update) | async-done | bytes 1048592 | tf_op jit(solution)/shard_map/reduce_scatter | solution.py:205
  1129.1 79.5 %reduce-scatter.17.cloned.1.call-done = bf16[256,2048]{1,0:T(8,128)(2,1)} async-done(((bf16[1024,2048]{1,0:T(8,128)(2,1)}), bf16[256,2048]{1,0:T(8,128)(2,1)}) %reduce-scatter.17.cloned.1.call-update) | async-done | bytes 1048592 | tf_op jit(solution)/shard_map/reduce_scatter | solution.py:205
  1218.9 15.5 fusion.190
  1234.4 14.7 add_convert_fusion.1
  1249.2 17.9 fusion.124
  1267.1 21.3 %add_convert_fusion = bf16[2048,2048]{1,0:T(8,128)(2,1)} fusion(f32[2048,2048]{1,0:T(8,128)} %fusion.124, bf16[1,1024,2048]{2,1,0:T(8,128)(2,1)S(1)} %copy-done.106, f32[1024,2048]{1,0:T(8,128)} %fusion.181, f32[2048]{0:T(1024)S(1)} %convert_element_type.266), kind=kOutput, calls=%fused_computation.128 | convolution fusion | flops 8619294720 | bytes 37756928 | tf_op jit(solution)/shard_map/dot_general | solution.py:50
  1288.5 10.6 all-gather.39.cloned.1.call-done
  1306.4 122.1 %while.59 = (s32[]{:T(128)}, f32[1024,8,64]{0,2,1:T(8,128)}, f32[1024,8,64]{0,2,1:T(8,128)}, bf16[2,512,512]{1,2,0:T(8,128)(2,1)}, s32[2]{0:T(128)S(1)}, /*index...) while((s32[]{:T(128)}, f32[1024,8,64]{0,2,1:T(8,128)}, ...), condition=%wide.region_34.35_spmd.clone, body=%wide.region_32.34_spmd.clone.sunk | while | flops 2738100736 | bytes 252303984 | solution.py:268
  1320.1 14.8 multiply_reduce_fusion.9
  1337.1 10.5 multiply_convert_fusion.8
  1379.8 15.5 multiply_reduce_fusion.9
  1398.2 10.6 multiply_convert_fusion.8
  1438.5 122.9 %while.58 = (s32[]{:T(128)}, f32[1024,8,64]{0,2,1:T(8,128)}, f32[1024,8,64]{0,2,1:T(8,128)}, bf16[2,512,512]{1,2,0:T(8,128)(2,1)}, s32[2]{0:T(128)S(1)}, /*index...) while((s32[]{:T(128)}, f32[1024,8,64]{0,2,1:T(8,128)}, ...), condition=%wide.region_25.26_spmd.clone, body=%wide.region_23.25_spmd.clone.sunk | while | flops 2738100736 | bytes 252303984 | solution.py:268
  1452.1 15.3 multiply_reduce_fusion.8
  1470.3 11.2 multiply_convert_fusion.7
  1514.8 14.8 multiply_reduce_fusion.8
  1641.3 22.2 %all-reduce.1 = (f32[512]{0:T(512)}, f32[512]{0:T(512)}, f32[2048]{0:T(1024)}) all-reduce(f32[512]{0:T(512)S(1)} %add_multiply_fusion, f32[512]{0:T(512)S(1)} %add.506, f32[2048]{0:T(1024)S(1)} %add.510), channel_id=1, replica_groups=mesh['dp'=8,'mp'=4] {'dp'}, use_global_device_ids=true, to_apply=%region_42.43 | all-reduce | flops 3072 | bytes 24576 | tf_op jit(solution)/shard_map/psum | solution.py:327
  1667.2 35.3 %reduce-scatter.35.cloned.1.call-done = bf16[256,512]{1,0:T(8,128)(2,1)} async-done(((bf16[2048,512]{1,0:T(8,128)(2,1)}), bf16[256,512]{1,0:T(8,128)(2,1)}) %reduce-scatter.35.cloned.1.call-update) | async-done | bytes 262160 | tf_op jit(solution)/shard_map/reduce_scatter | solution.py:314
  1704.3 42.9 %reduce-scatter.37.cloned.1.call-done = bf16[512,256]{1,0:T(8,128)(2,1)} async-done(((bf16[512,2048]{1,0:T(8,128)(2,1)}), bf16[512,256]{1,0:T(8,128)(2,1)}) %reduce-scatter.37.cloned.1.call-update) | async-done | bytes 262160 | tf_op jit(solution)/shard_map/reduce_scatter | solution.py:317
  1749.0 77.2 %reduce-scatter.25.cloned.1.call-done = bf16[256,2048]{1,0:T(8,128)(2,1)} async-done(((bf16[1024,2048]{1,0:T(8,128)(2,1)}), bf16[256,2048]{1,0:T(8,128)(2,1)}) %reduce-scatter.25.cloned.1.call-update) | async-done | bytes 1048592 | tf_op jit(solution)/shard_map/reduce_scatter | solution.py:279
  1828.4 78.0 %reduce-scatter.29.cloned.1.call-done = bf16[256,2048]{1,0:T(8,128)(2,1)} async-done(((bf16[1024,2048]{1,0:T(8,128)(2,1)}), bf16[256,2048]{1,0:T(8,128)(2,1)}) %reduce-scatter.29.cloned.1.call-update) | async-done | bytes 1048592 | tf_op jit(solution)/shard_map/reduce_scatter | solution.py:279
  1916.6 41.8 %all-reduce = (f32[2048]{0:T(1024)}, f32[2048]{0:T(1024)}, f32[2048]{0:T(1024)}, f32[2048]{0:T(1024)}, f32[2048]{0:T(1024)}, /*index=5*/f32[2048]{0:T(1024)}) all-reduce(f32[2048]{0:T(1024)S(1)} %add.508, f32[2048]{0:T(1024)S(1)} %add.512, f32[2048]{0:T(1024)S(1)} %add.513, ...), channel_id=1, replica_groups=mesh['dp'=8,'mp'=4] {'dp','mp'}, use_global_device_ids=true, to_apply=%region_51.52 | all-reduce | flops 12288 | bytes 98304 | tf_op jit(solution)/shard_map/psum | solution.py:328
  1962.4 81.9 %all-reduce.4.cloned.1.call-done = f32[50,2048]{1,0:T(8,128)} async-done(((f32[50,2048]{1,0:T(8,128)}), f32[50,2048]{1,0:T(8,128)}) %all-reduce.4.cloned.1.call-update) | async-done | bytes 409616 | tf_op jit(solution)/shard_map/psum | solution.py:328
  (563 shorter events, 411.9 us)
Async XLA Ops:
  7.2 33.2 %all-gather.21.cloned.1.call-start = ((), (), s32[]{:S(2)}) async-start(), calls=%async_computation.16 | async-start | bytes 2359296 | tf_op jit(solution)/shard_map/all_gather | solution.py:141
  7.9 114.9 %all-gather.17.cloned.1.call-start = ((), (), s32[]{:S(2)}) async-start(), calls=%async_computation.14 | async-start | bytes 5242880 | tf_op jit(solution)/shard_map/all_gather | solution.py:151
  14.1 137.6 %all-gather.19.cloned.1.call-start = ((), (), s32[]{:S(2)}) async-start(), calls=%async_computation.15 | async-start | bytes 2359296 | tf_op jit(solution)/shard_map/all_gather | solution.py:140
  14.8 166.5 %all-gather.23.cloned.1.call-start = ((), (), s32[]{:S(2)}) async-start(), calls=%async_computation.17 | async-start | bytes 2359296 | tf_op jit(solution)/shard_map/all_gather | solution.py:142
  15.4 206.4 %all-gather.25.cloned.1.call-start = ((), (), s32[]{:S(2)}) async-start(), calls=%async_computation.18 | async-start | bytes 2359296 | tf_op jit(solution)/shard_map/all_gather | solution.py:143
  16.0 277.8 %all-gather.33.cloned.1.call-start = ((), (), s32[]{:S(2)}) async-start(), calls=%async_computation.24 | async-start | bytes 5242880 | tf_op jit(solution)/shard_map/all_gather | solution.py:151
  16.6 355.3 %reduce-scatter.15.cloned.1.call-start = ((), (), s32[]{:S(2)}) async-start(), calls=%async_computation.19 | async-start | bytes 5242880 | tf_op jit(solution)/shard_map/reduce_scatter | solution.py:184
  16.6 135.0 %copy-start.95 = (f32[512]{0:T(512)}, f32[512]{0:T(512)S(1)}, u32[]{:S(2)}) copy-start(f32[512]{0:T(512)S(1)} %convert_element_type.257) | copy-start | bytes 6148
  16.7 164.7 %copy-start.93 = (f32[512]{0:T(512)}, f32[512]{0:T(512)S(1)}, u32[]{:S(2)}) copy-start(f32[512]{0:T(512)S(1)} %convert_element_type.260) | copy-start | bytes 6148
  228.9 64.8 %copy-start.96 = (f32[512]{0:T(512)S(1)}, f32[512]{0:T(512)}, u32[]{:S(2)}) copy-start(f32[512]{0:T(512)} %copy-done.95) | copy-start | bytes 6148
  229.0 222.6 %reduce-scatter.19.cloned.1.call-start = ((), (), s32[]{:S(2)}) async-start(), calls=%async_computation.25 | async-start | bytes 5242880 | tf_op jit(solution)/shard_map/reduce_scatter | solution.py:184
  348.2 103.4 %copy-start.15 = (f32[256,2048]{1,0:T(8,128)S(1)}, f32[256,2048]{1,0:T(8,128)}, u32[]{:S(2)}) copy-start(f32[256,2048]{1,0:T(8,128)} %copy-done.14) | copy-start | bytes 6291460
  348.3 160.6 %all-gather.29.cloned.1.call-start = ((), (), s32[]{:S(2)}) async-start(), calls=%async_computation.21 | async-start | bytes 9437184 | tf_op jit(solution)/shard_map/all_gather | solution.py:144
  349.0 242.2 %all-gather.27.cloned.1.call-start = ((), (), s32[]{:S(2)}) async-start(), calls=%async_computation.20 | async-start | bytes 5242880 | tf_op jit(solution)/shard_map/all_gather | solution.py:193
  457.4 215.3 %all-gather.41.cloned.1.call-start = ((), (), s32[]{:S(2)}) async-start(), calls=%async_computation.41 | async-start | bytes 5242880 | tf_op jit(solution)/shard_map/all_gather | solution.py:213
  459.7 269.6 %all-gather.31.cloned.1.call-start = ((), (), s32[]{:S(2)}) async-start(), calls=%async_computation.22 | async-start | bytes 9437184 | tf_op jit(solution)/shard_map/all_gather | solution.py:145
  460.3 351.0 %all-gather.35.cloned.1.call-start = ((), (), s32[]{:S(2)}) async-start(), calls=%async_computation.26 | async-start | bytes 5242880 | tf_op jit(solution)/shard_map/all_gather | solution.py:193
  461.0 431.0 %all-gather.43.cloned.1.call-start = ((), (), s32[]{:S(2)}) async-start(), calls=%async_computation.42 | async-start | bytes 5242880 | tf_op jit(solution)/shard_map/all_gather | solution.py:213
  461.6 508.5 %reduce-scatter.23.cloned.1.call-start = ((), (), s32[]{:S(2)}) async-start(), calls=%async_computation.28 | async-start | bytes 5242880 | tf_op jit(solution)/shard_map/reduce_scatter | solution.py:223
  763.2 286.4 %reduce-scatter.27.cloned.1.call-start = ((), (), s32[]{:S(2)}) async-start(), calls=%async_computation.31 | async-start | bytes 5242880 | tf_op jit(solution)/shard_map/reduce_scatter | solution.py:223
  926.2 202.9 %reduce-scatter.21.cloned.1.call-start = ((), (), s32[]{:S(2)}) async-start(), calls=%async_computation.27 | async-start | bytes 5242880 | tf_op jit(solution)/shard_map/reduce_scatter | solution.py:205
  942.4 266.2 %reduce-scatter.17.cloned.1.call-start = ((), (), s32[]{:S(2)}) async-start(), calls=%async_computation.23 | async-start | bytes 5242880 | tf_op jit(solution)/shard_map/reduce_scatter | solution.py:205
  958.6 91.0 %copy-start.22 = (f32[256,2048]{1,0:T(8,128)S(1)}, f32[256,2048]{1,0:T(8,128)}, u32[]{:S(2)}) copy-start(f32[256,2048]{1,0:T(8,128)} %copy-done.21) | copy-start | bytes 6291460
  958.7 91.0 %copy-start.61 = (f32[2048]{0:T(1024)S(1)}, f32[2048]{0:T(1024)}, u32[]{:S(2)}) copy-start(f32[2048]{0:T(1024)} %param.43) | copy-start | bytes 24580
  958.7 91.0 %copy-start.73 = (f32[256]{0:T(256)S(1)}, f32[256]{0:T(256)}, u32[]{:S(2)}) copy-start(f32[256]{0:T(256)} %copy-done.72) | copy-start | bytes 3076
  958.7 91.0 %copy-start.75 = (f32[256]{0:T(256)S(1)}, f32[256]{0:T(256)}, u32[]{:S(2)}) copy-start(f32[256]{0:T(256)} %copy-done.74) | copy-start | bytes 3076
  958.7 91.0 %copy-start.81 = (f32[256]{0:T(256)S(1)}, f32[256]{0:T(256)}, u32[]{:S(2)}) copy-start(f32[256]{0:T(256)} %copy-done.80) | copy-start | bytes 3076
  958.7 91.0 %copy-start.83 = (f32[256]{0:T(256)S(1)}, f32[256]{0:T(256)}, u32[]{:S(2)}) copy-start(f32[256]{0:T(256)} %copy-done.82) | copy-start | bytes 3076
  958.7 340.3 %all-gather.39.cloned.1.call-start = ((), (), s32[]{:S(2)}) async-start(), calls=%async_computation.32 | async-start | bytes 5242880 | tf_op jit(solution)/shard_map/all_gather | solution.py:227
  1217.6 213.4 %all-gather.37.cloned.1.call-start = ((), (), s32[]{:S(2)}) async-start(), calls=%async_computation.29 | async-start | bytes 5242880 | tf_op jit(solution)/shard_map/all_gather | solution.py:227
  1218.8 413.9 %reduce-scatter.39.cloned.1.call-start = ((), (), s32[]{:S(2)}) async-start(), calls=%async_computation.39 | async-start | bytes 9437184 | tf_op jit(solution)/shard_map/reduce_scatter | solution.py:320
  1249.1 386.4 %reduce-scatter.41.cloned.1.call-start = ((), (), s32[]{:S(2)}) async-start(), calls=%async_computation.40 | async-start | bytes 9437184 | tf_op jit(solution)/shard_map/reduce_scatter | solution.py:323
  1288.4 375.1 %reduce-scatter.31.cloned.1.call-start = ((), (), s32[]{:S(2)}) async-start(), calls=%async_computation.35 | async-start | bytes 2359296 | tf_op jit(solution)/shard_map/reduce_scatter | solution.py:308
  1572.0 93.3 %reduce-scatter.33.cloned.1.call-start = ((), (), s32[]{:S(2)}) async-start(), calls=%async_computation.36 | async-start | bytes 2359296 | tf_op jit(solution)/shard_map/reduce_scatter | solution.py:311
  1582.5 119.9 %reduce-scatter.35.cloned.1.call-start = ((), (), s32[]{:S(2)}) async-start(), calls=%async_computation.37 | async-start | bytes 2359296 | tf_op jit(solution)/shard_map/reduce_scatter | solution.py:314
  1593.3 153.9 %reduce-scatter.37.cloned.1.call-start = ((), (), s32[]{:S(2)}) async-start(), calls=%async_computation.38 | async-start | bytes 2359296 | tf_op jit(solution)/shard_map/reduce_scatter | solution.py:317
  1601.9 224.3 %reduce-scatter.25.cloned.1.call-start = ((), (), s32[]{:S(2)}) async-start(), calls=%async_computation.30 | async-start | bytes 5242880 | tf_op jit(solution)/shard_map/reduce_scatter | solution.py:279
  1614.4 292.1 %reduce-scatter.29.cloned.1.call-start = ((), (), s32[]{:S(2)}) async-start(), calls=%async_computation.33 | async-start | bytes 5242880 | tf_op jit(solution)/shard_map/reduce_scatter | solution.py:279
  1627.5 416.8 %all-reduce.4.cloned.1.call-start = ((), (), s32[]{:S(2)}) async-start(), calls=%async_computation.34 | async-start | bytes 917504 | tf_op jit(solution)/shard_map/psum | solution.py:328
  1635.5 190.7 %copy-start.16 = (f32[256,2048]{1,0:T(8,128)S(1)}, f32[256,2048]{1,0:T(8,128)}, u32[]{:S(2)}) copy-start(f32[256,2048]{1,0:T(8,128)} %copy-done.14) | copy-start | bytes 6291460
  1635.5 190.7 %copy-start.59 = (f32[2048]{0:T(1024)S(1)}, f32[2048]{0:T(1024)}, u32[]{:S(2)}) copy-start(f32[2048]{0:T(1024)} %param.41) | copy-start | bytes 24580
  1635.5 190.7 %copy-start.69 = (f32[256]{0:T(256)S(1)}, f32[256]{0:T(256)}, u32[]{:S(2)}) copy-start(f32[256]{0:T(256)} %copy-done.68) | copy-start | bytes 3076
  1635.5 190.7 %copy-start.77 = (f32[256]{0:T(256)S(1)}, f32[256]{0:T(256)}, u32[]{:S(2)}) copy-start(f32[256]{0:T(256)} %copy-done.76) | copy-start | bytes 3076
  1638.5 268.0 %copy-start.71 = (f32[256]{0:T(256)S(1)}, f32[256]{0:T(256)}, u32[]{:S(2)}) copy-start(f32[256]{0:T(256)} %copy-done.70) | copy-start | bytes 3076
  1638.5 268.0 %copy-start.79 = (f32[256]{0:T(256)S(1)}, f32[256]{0:T(256)}, u32[]{:S(2)}) copy-start(f32[256]{0:T(256)} %copy-done.78) | copy-start | bytes 3076
  1828.4 83.2 %copy-start.85 = (s32[256]{0:T(256)S(1)}, s32[256]{0:T(256)}, u32[]{:S(2)}) copy-start(s32[256]{0:T(256)} %copy-done.84) | copy-start | bytes 3076
  1912.6 45.8 %copy-start.29 = (f32[256,2048]{1,0:T(8,128)S(1)}, f32[256,2048]{1,0:T(8,128)}, u32[]{:S(2)}) copy-start(f32[256,2048]{1,0:T(8,128)} %copy-done.28) | copy-start | bytes 6291460
  1958.4 87.7 %copy-start.1 = (f32[50,2048]{1,0:T(8,128)S(1)}, f32[50,2048]{1,0:T(8,128)}, u32[]{:S(2)}) copy-start(f32[50,2048]{1,0:T(8,128)} %param.29) | copy-start | bytes 1228804
  (133 other events, 852.0 us)
Sparse Core Ops, SparseCore 0:
  9.9 30.3 all-gather.20
  42.5 80.3 all-gather.16
  124.8 26.8 all-gather.18
  153.4 27.8 all-gather.22
  183.1 28.1 all-gather.24
  213.3 80.4 all-gather.32
  296.6 75.2 reduce-scatter.14
  374.3 77.2 reduce-scatter.18
  453.5 55.2 all-gather.28
  510.8 80.3 all-gather.26
  593.3 79.2 all-gather.40
  674.4 54.8 all-gather.30
  730.9 80.3 all-gather.34
  812.7 79.2 all-gather.42
  894.8 75.3 reduce-scatter.22
  972.4 77.2 reduce-scatter.26
  1051.8 77.2 reduce-scatter.20
  1131.3 77.2 reduce-scatter.16
  1217.7 81.2 all-gather.38
  1300.4 79.2 all-gather.36
  1383.2 69.7 reduce-scatter.38
  1456.9 71.2 reduce-scatter.40
  1572.2 40.9 reduce-scatter.30
  1616.6 41.3 reduce-scatter.32
  1661.3 41.1 reduce-scatter.34
  1706.0 41.2 reduce-scatter.36
  1749.4 76.7 reduce-scatter.24
  1829.2 77.2 reduce-scatter.28
  1916.7 127.5 all-reduce.3
where the time goes:
time: 2060 us; the launch traced here: 2050 us
  waiting for transfers between devices  1260 us (61%)
  matrix products  513 us (25%)
  other arithmetic  122 us (6%)
  blocking collectives  64 us (3%)
  local copies, waits for them, and re-layouts  56.1 us (3%)
    reduce_scatter x2, waiting for transfers between devices, shards(): lax.psum_scatter((times_t(grad_query, query_full) * qk_scale + times_t(gr...  155 us
    reduce_scatter x2, waiting for transfers between devices, shards(): lax.psum_scatter(dense(active, down_full).astype(jnp.bfloat16), 'mp', sca...  155 us
    all_gather x2, waiting for transfers between devices, shards(): lax.all_gather(normed.astype(jnp.bfloat16), 'mp', axis=0, tiled=True)  147 us
    all_gather x2, waiting for transfers between devices, shards(): mlp_shard_rows = lax.all_gather(grad_rows, 'mp', axis=0, tiled=True)  133 us
    all_gather x2, waiting for transfers between devices, shards(): lax.all_gather(normed_two.astype(jnp.bfloat16), 'mp', axis=0, tiled=True)  130 us
    dot_general x12, matrix products, dense(): return jnp.dot(left_side, right_side, preferred_element_type=jnp.float32)  105 us
    reduce_scatter x2, waiting for transfers between devices, shards(): lax.psum_scatter(dense(attended, out_full).astype(jnp.bfloat16), 'mp', sc...  103 us
    dot_general x12, matrix products, times_t(): lax.dot_general(left_side, right_side, (((1,), (1,)), ((), ())), preferre...  101 us
  transfers between devices with their start and end apart: 29, of which 23 were waited for; matrix products, arithmetic and copies ran while one was open for 31% of the time, Pallas kernels for 0%

commit v1 on v0

--- a/solution.py
+++ b/solution.py
@@ -326,8 +326,19 @@
     )
     head_total = lax.psum((head_sums[0], head_sums[1], head_sums[2]), "dp")
     row_total = lax.psum(
-        (row_sums[0], row_sums[1], row_sums[2], row_sums[3], row_sums[4], row_sums[5], row_sums[6]),
-        ("dp", "mp"),
+        lax.psum(
+            (
+                row_sums[0],
+                row_sums[1],
+                row_sums[2],
+                row_sums[3],
+                row_sums[4],
+                row_sums[5],
+                row_sums[6],
+            ),
+            "mp",
+        ),
+        "dp",
     )
     return (
         jnp.stack(outputs),

time: 2060 us -> 1980 us (0.961)
  waiting for transfers between devices: 1260 us -> 1190 us
  blocking collectives: 64 us -> 41.8 us
    reduce_scatter x2, waiting for transfers between devices: 155 us -> 32.3 us  [shards(): lax.psum_scatter((times_t(grad_query, query_full) * qk_scale + times_t(gr...]
    psum x1, waiting for transfers between devices: 81.9 us -> 0.01 us  [shards(): lax.psum((row_sums[0], row_sums[1], row_sums[2], row_sums[3], row_sums[4]...]
    psum x0 -> x1, waiting for transfers between devices: none -> 49.8 us  [shards(): lax.psum(lax.psum((row_sums[0], row_sums[1], row_sums[2], row_sums[3], ro...]
    reduce_scatter x1, waiting for transfers between devices: 0.01 us -> 43.1 us  [shards(): lax.psum_scatter(full_sums[0].astype(jnp.bfloat16), 'dp', scatter_dimensi...]
    reduce_scatter x1, waiting for transfers between devices: 0.01 us -> 42.6 us  [shards(): lax.psum_scatter(full_sums[1].astype(jnp.bfloat16), 'dp', scatter_dimensi...]
    psum x1, blocking collectives: 41.8 us -> 16.3 us  [shards(): lax.psum((row_sums[0], row_sums[1], row_sums[2], row_sums[3], row_sums[4]...]
  transfers between devices with their start and end apart: 29 -> 30, of which waited for: 23 -> 24; matrix products, arithmetic and copies ran while one was open for 31% -> 34% of each run, Pallas kernels for 0% -> 0%
where the time goes in v1:
time: 1980 us; the launch traced here: 1970 us
  waiting for transfers between devices  1190 us (60%)
  matrix products  531 us (27%)
  other arithmetic  124 us (6%)
  local copies, waits for them, and re-layouts  50.3 us (3%)
  blocking collectives  41.8 us (2%)
    reduce_scatter x2, waiting for transfers between devices, shards(): lax.psum_scatter(dense(active, down_full).astype(jnp.bfloat16), 'mp', sca...  155 us
    all_gather x2, waiting for transfers between devices, shards(): lax.all_gather(normed.astype(jnp.bfloat16), 'mp', axis=0, tiled=True)  148 us
    all_gather x2, waiting for transfers between devices, shards(): mlp_shard_rows = lax.all_gather(grad_rows, 'mp', axis=0, tiled=True)  132 us
    all_gather x2, waiting for transfers between devices, shards(): lax.all_gather(normed_two.astype(jnp.bfloat16), 'mp', axis=0, tiled=True)  131 us
    reduce_scatter x2, waiting for transfers between devices, shards(): lax.psum_scatter(dense(attended, out_full).astype(jnp.bfloat16), 'mp', sc...  104 us
    dot_general x12, matrix products, dense(): return jnp.dot(left_side, right_side, preferred_element_type=jnp.float32)  104 us
    dot_general x12, matrix products, inner_rows(): lax.dot_general(left_side, right_side, (((0,), (0,)), ((), ())), preferre...  103 us
    dot_general x12, matrix products, times_t(): lax.dot_general(left_side, right_side, (((1,), (1,)), ((), ())), preferre...  100 us
  transfers between devices with their start and end apart: 30, of which 24 were waited for; matrix products, arithmetic and copies ran while one was open for 34% of the time, Pallas kernels for 0%

profile of v1, /device:TPU:1, one launch (start us, length us, event | category | flops | bytes accessed | tf_op | source)
XLA Modules:
  0.0 1973.6 jit_solution(14341466282499038694)
XLA Ops:
  17.4 23.0 %all-gather.21.cloned.1.call-done = bf16[2048,512]{1,0:T(8,128)(2,1)} async-done(((bf16[256,512]{1,0:T(8,128)(2,1)}), bf16[2048,512]{1,0:T(8,128)(2,1)}) %all-gather.21.cloned.1.call-update) | async-done | bytes 2097168 | tf_op jit(solution)/shard_map/all_gather | solution.py:141
  40.4 82.5 %all-gather.33.cloned.1.call-done = bf16[1024,2048]{1,0:T(8,128)(2,1)} async-done(((bf16[256,2048]{1,0:T(8,128)(2,1)}), bf16[1024,2048]{1,0:T(8,128)(2,1)}) %all-gather.33.cloned.1.call-update) | async-done | bytes 4194320 | tf_op jit(solution)/shard_map/all_gather | solution.py:151
  129.1 22.6 %all-gather.23.cloned.1.call-done = bf16[2048,512]{1,0:T(8,128)(2,1)} async-done(((bf16[256,512]{1,0:T(8,128)(2,1)}), bf16[2048,512]{1,0:T(8,128)(2,1)}) %all-gather.23.cloned.1.call-update) | async-done | bytes 2097168 | tf_op jit(solution)/shard_map/all_gather | solution.py:142
  156.9 24.4 %all-gather.19.cloned.1.call-done = bf16[2048,512]{1,0:T(8,128)(2,1)} async-done(((bf16[256,512]{1,0:T(8,128)(2,1)}), bf16[2048,512]{1,0:T(8,128)(2,1)}) %all-gather.19.cloned.1.call-update) | async-done | bytes 2097168 | tf_op jit(solution)/shard_map/all_gather | solution.py:140
  188.6 32.4 %while.57 = (s32[]{:T(128)}, bf16[2,512,512]{2,1,0:T(8,128)(2,1)}, f32[2,8,512]{2,1,0:T(8,128)S(1)}, s32[2]{0:T(128)S(1)}, bf16[1024,8,64]{0,2,1:T(8,128)(2,1)},...) while((s32[]{:T(128)}, bf16[2,512,512]{2,1,0:T(8,128)(2,1)}, ...), condition=%wide.region_15.16_spmd.clone, body=%wide.region_12.15_spmd.clone.sunk | while | flops 1112807936 | bytes 57809596 | solution.py:180
  228.3 65.3 %all-gather.17.cloned.1.call-done = bf16[1024,2048]{1,0:T(8,128)(2,1)} async-done(((bf16[256,2048]{1,0:T(8,128)(2,1)}), bf16[1024,2048]{1,0:T(8,128)(2,1)}) %all-gather.17.cloned.1.call-update) | async-done | bytes 4194320 | tf_op jit(solution)/shard_map/all_gather | solution.py:151
  306.3 32.7 %while.56 = (s32[]{:T(128)}, bf16[2,512,512]{2,1,0:T(8,128)(2,1)}, f32[2,8,512]{2,1,0:T(8,128)S(1)}, s32[2]{0:T(128)S(1)}, bf16[1024,8,64]{0,2,1:T(8,128)(2,1)},...) while((s32[]{:T(128)}, bf16[2,512,512]{2,1,0:T(8,128)(2,1)}, ...), condition=%wide.region_5.6_spmd.clone, body=%wide.region_2.5_spmd.clone.sunk | while | flops 1112807936 | bytes 57809596 | solution.py:180
  347.3 24.1 %reduce-scatter.19.cloned.1.call-done = bf16[256,2048]{1,0:T(8,128)(2,1)} async-done(((bf16[1024,2048]{1,0:T(8,128)(2,1)}), bf16[256,2048]{1,0:T(8,128)(2,1)}) %reduce-scatter.19.cloned.1.call-update) | async-done | bytes 1048592 | tf_op jit(solution)/shard_map/reduce_scatter | solution.py:184
  371.4 80.3 %reduce-scatter.15.cloned.1.call-done = bf16[256,2048]{1,0:T(8,128)(2,1)} async-done(((bf16[1024,2048]{1,0:T(8,128)(2,1)}), bf16[256,2048]{1,0:T(8,128)(2,1)}) %reduce-scatter.15.cloned.1.call-update) | async-done | bytes 1048592 | tf_op jit(solution)/shard_map/reduce_scatter | solution.py:184
  461.8 47.1 %all-gather.29.cloned.1.call-done = bf16[2048,2048]{1,0:T(8,128)(2,1)} async-done(((bf16[256,2048]{1,0:T(8,128)(2,1)}), bf16[2048,2048]{1,0:T(8,128)(2,1)}) %all-gather.29.cloned.1.call-update) | async-done | bytes 8388624 | tf_op jit(solution)/shard_map/all_gather | solution.py:144
  508.9 82.4 %all-gather.35.cloned.1.call-done = bf16[1024,2048]{1,0:T(8,128)(2,1)} async-done(((bf16[256,2048]{1,0:T(8,128)(2,1)}), bf16[1024,2048]{1,0:T(8,128)(2,1)}) %all-gather.35.cloned.1.call-update) | async-done | bytes 4194320 | tf_op jit(solution)/shard_map/all_gather | solution.py:193
  591.2 14.7 fusion.181
  606.0 66.2 %all-gather.43.cloned.1.call-done = bf16[1,1024,2048]{2,1,0:T(8,128)(2,1)} async-done(((bf16[1,256,2048]{2,1,0:T(8,128)(2,1)}), bf16[1,1024,2048]{2,1,0:T(8,128)(2,1)}) %all-gather.43.cloned.1.call-update) | async-done | bytes 4194320 | tf_op jit(solution)/shard_map/all_gather | solution.py:213
  672.1 56.7 %all-gather.31.cloned.1.call-done = bf16[2048,2048]{1,0:T(8,128)(2,1)} async-done(((bf16[2048,256]{1,0:T(8,128)(2,1)}), bf16[2048,2048]{1,0:T(8,128)(2,1)}) %all-gather.31.cloned.1.call-update) | async-done | bytes 8388624 | tf_op jit(solution)/shard_map/all_gather | solution.py:145
  728.8 18.7 convert_reduce_fusion
  749.6 13.1 convolution_convert_fusion.2
  762.8 48.5 %all-gather.27.cloned.1.call-done = bf16[1024,2048]{1,0:T(8,128)(2,1)} async-done(((bf16[256,2048]{1,0:T(8,128)(2,1)}), bf16[1024,2048]{1,0:T(8,128)(2,1)}) %all-gather.27.cloned.1.call-update) | async-done | bytes 4194320 | tf_op jit(solution)/shard_map/all_gather | solution.py:193
  811.3 14.5 fusion.180
  825.9 66.2 %all-gather.41.cloned.1.call-done = bf16[1,1024,2048]{2,1,0:T(8,128)(2,1)} async-done(((bf16[1,256,2048]{2,1,0:T(8,128)(2,1)}), bf16[1,1024,2048]{2,1,0:T(8,128)(2,1)}) %all-gather.41.cloned.1.call-update) | async-done | bytes 4194320 | tf_op jit(solution)/shard_map/all_gather | solution.py:213
  892.1 18.9 convert_reduce_fusion.1
  913.0 13.2 convolution_convert_fusion.3
  926.2 16.2 convolution_convert_fusion.6
  942.4 16.2 convolution_convert_fusion.4
  969.6 80.2 %reduce-scatter.23.cloned.1.call-done = bf16[256,2048]{1,0:T(8,128)(2,1)} async-done(((bf16[1024,2048]{1,0:T(8,128)(2,1)}), bf16[256,2048]{1,0:T(8,128)(2,1)}) %reduce-scatter.23.cloned.1.call-update) | async-done | bytes 1048592 | tf_op jit(solution)/shard_map/reduce_scatter | solution.py:223
  1053.9 75.2 %reduce-scatter.17.cloned.1.call-done = bf16[256,2048]{1,0:T(8,128)(2,1)} async-done(((bf16[1024,2048]{1,0:T(8,128)(2,1)}), bf16[256,2048]{1,0:T(8,128)(2,1)}) %reduce-scatter.17.cloned.1.call-update) | async-done | bytes 1048592 | tf_op jit(solution)/shard_map/reduce_scatter | solution.py:205
  1129.2 79.5 %reduce-scatter.21.cloned.1.call-done = bf16[256,2048]{1,0:T(8,128)(2,1)} async-done(((bf16[1024,2048]{1,0:T(8,128)(2,1)}), bf16[256,2048]{1,0:T(8,128)(2,1)}) %reduce-scatter.21.cloned.1.call-update) | async-done | bytes 1048592 | tf_op jit(solution)/shard_map/reduce_scatter | solution.py:205
  1219.4 15.5 fusion.190
  1234.9 14.7 add_convert_fusion.1
  1249.6 17.9 fusion.124
  1267.5 21.3 %add_convert_fusion = bf16[2048,2048]{1,0:T(8,128)(2,1)} fusion(f32[2048,2048]{1,0:T(8,128)} %fusion.124, bf16[1,1024,2048]{2,1,0:T(8,128)(2,1)S(1)} %copy-done.93, f32[1024,2048]{1,0:T(8,128)} %fusion.181, f32[2048]{0:T(1024)S(1)} %convert_element_type.266), kind=kOutput, calls=%fused_computation.128 | convolution fusion | flops 8619294720 | bytes 37756928 | tf_op jit(solution)/shard_map/dot_general | solution.py:50
  1288.9 10.6 all-gather.37.cloned.1.call-done
  1306.2 127.9 %while.58 = (s32[]{:T(128)}, f32[1024,8,64]{0,2,1:T(8,128)}, f32[1024,8,64]{0,2,1:T(8,128)}, bf16[2,512,512]{1,2,0:T(8,128)(2,1)}, s32[2]{0:T(128)S(1)}, /*index...) while((s32[]{:T(128)}, f32[1024,8,64]{0,2,1:T(8,128)}, ...), condition=%wide.region_25.26_spmd.clone, body=%wide.region_23.25_spmd.clone.sunk | while | flops 2738100736 | bytes 248110096 | solution.py:268
  1320.4 14.8 multiply_reduce_fusion.8
  1381.7 15.6 multiply_reduce_fusion.8
  1400.4 11.1 multiply_convert_fusion.7
  1461.2 130.0 %while.59 = (s32[]{:T(128)}, f32[1024,8,64]{0,2,1:T(8,128)}, f32[1024,8,64]{0,2,1:T(8,128)}, bf16[2,512,512]{1,2,0:T(8,128)(2,1)}, s32[2]{0:T(128)S(1)}, /*index...) while((s32[]{:T(128)}, f32[1024,8,64]{0,2,1:T(8,128)}, ...), condition=%wide.region_34.35_spmd.clone, body=%wide.region_32.34_spmd.clone.sunk | while | flops 2738100736 | bytes 248110096 | solution.py:268
  1462.8 12.0 fusion.341
  1477.9 15.2 multiply_reduce_fusion.9
  1496.2 10.8 multiply_convert_fusion.8
  1541.9 14.8 multiply_reduce_fusion.9
  1655.6 32.3 %reduce-scatter.29.cloned.1.call-done = bf16[256,2048]{1,0:T(8,128)(2,1)} async-done(((bf16[1024,2048]{1,0:T(8,128)(2,1)}), bf16[256,2048]{1,0:T(8,128)(2,1)}) %reduce-scatter.29.cloned.1.call-update) | async-done | bytes 1048592 | tf_op jit(solution)/shard_map/reduce_scatter | solution.py:279
  1701.2 31.8 %reduce-scatter.37.cloned.1.call-done = bf16[512,256]{1,0:T(8,128)(2,1)} async-done(((bf16[512,2048]{1,0:T(8,128)(2,1)}), bf16[512,256]{1,0:T(8,128)(2,1)}) %reduce-scatter.37.cloned.1.call-update) | async-done | bytes 262160 | tf_op jit(solution)/shard_map/reduce_scatter | solution.py:317
  1734.7 43.0 %reduce-scatter.35.cloned.1.call-done = bf16[256,512]{1,0:T(8,128)(2,1)} async-done(((bf16[2048,512]{1,0:T(8,128)(2,1)}), bf16[256,512]{1,0:T(8,128)(2,1)}) %reduce-scatter.35.cloned.1.call-update) | async-done | bytes 262160 | tf_op jit(solution)/shard_map/reduce_scatter | solution.py:314
  1779.5 42.6 %reduce-scatter.33.cloned.1.call-done = bf16[256,512]{1,0:T(8,128)(2,1)} async-done(((bf16[2048,512]{1,0:T(8,128)(2,1)}), bf16[256,512]{1,0:T(8,128)(2,1)}) %reduce-scatter.33.cloned.1.call-update) | async-done | bytes 262160 | tf_op jit(solution)/shard_map/reduce_scatter | solution.py:311
  1823.9 43.1 %reduce-scatter.31.cloned.1.call-done = bf16[256,512]{1,0:T(8,128)(2,1)} async-done(((bf16[2048,512]{1,0:T(8,128)(2,1)}), bf16[256,512]{1,0:T(8,128)(2,1)}) %reduce-scatter.31.cloned.1.call-update) | async-done | bytes 262160 | tf_op jit(solution)/shard_map/reduce_scatter | solution.py:308
  1868.8 16.3 all-reduce.1
  1885.1 25.5 %all-reduce = (f32[512]{0:T(512)}, f32[512]{0:T(512)}, f32[2048]{0:T(1024)}, f32[2048]{0:T(1024)}, f32[2048]{0:T(1024)}, /*index=5*/f32[2048]{0:T(1024)}, f32[2048]{0:T(1024)}, f32[2048]{0:T(1024)}, f32[2048]{0:T(1024)}) all-reduce(f32[512]{0:T(512)S(1)} %add_multiply_fusion, ...), channel_id=1, replica_groups=mesh['dp'=8,'mp'=4] {'dp'}, use_global_device_ids=true, to_apply=%region_43.44 | all-reduce | flops 15360 | bytes 122880 | tf_op jit(solution)/shard_map/psum | solution.py:327
  1914.7 49.8 %all-reduce.7.cloned.1.call-done = f32[50,2048]{1,0:T(8,128)} async-done(((f32[50,2048]{1,0:T(8,128)}), f32[50,2048]{1,0:T(8,128)}) %all-reduce.7.cloned.1.call-update) | async-done | bytes 409616 | tf_op jit(solution)/shard_map/psum | solution.py:328
  (538 shorter events, 434.2 us)
Async XLA Ops:
  7.2 33.2 %all-gather.21.cloned.1.call-start = ((), (), s32[]{:S(2)}) async-start(), calls=%async_computation.16 | async-start | bytes 2359296 | tf_op jit(solution)/shard_map/all_gather | solution.py:141
  7.9 114.9 %all-gather.33.cloned.1.call-start = ((), (), s32[]{:S(2)}) async-start(), calls=%async_computation.24 | async-start | bytes 5242880 | tf_op jit(solution)/shard_map/all_gather | solution.py:151
  14.1 137.6 %all-gather.23.cloned.1.call-start = ((), (), s32[]{:S(2)}) async-start(), calls=%async_computation.17 | async-start | bytes 2359296 | tf_op jit(solution)/shard_map/all_gather | solution.py:142
  14.8 166.5 %all-gather.19.cloned.1.call-start = ((), (), s32[]{:S(2)}) async-start(), calls=%async_computation.15 | async-start | bytes 2359296 | tf_op jit(solution)/shard_map/all_gather | solution.py:140
  15.4 205.7 %all-gather.25.cloned.1.call-start = ((), (), s32[]{:S(2)}) async-start(), calls=%async_computation.18 | async-start | bytes 2359296 | tf_op jit(solution)/shard_map/all_gather | solution.py:143
  16.0 277.7 %all-gather.17.cloned.1.call-start = ((), (), s32[]{:S(2)}) async-start(), calls=%async_computation.14 | async-start | bytes 5242880 | tf_op jit(solution)/shard_map/all_gather | solution.py:151
  16.6 354.8 %reduce-scatter.19.cloned.1.call-start = ((), (), s32[]{:S(2)}) async-start(), calls=%async_computation.25 | async-start | bytes 5242880 | tf_op jit(solution)/shard_map/reduce_scatter | solution.py:184
  16.7 135.0 %copy-start.82 = (f32[512]{0:T(512)}, f32[512]{0:T(512)S(1)}, u32[]{:S(2)}) copy-start(f32[512]{0:T(512)S(1)} %convert_element_type.260) | copy-start | bytes 6148
  16.7 164.6 %copy-start.84 = (f32[512]{0:T(512)}, f32[512]{0:T(512)S(1)}, u32[]{:S(2)}) copy-start(f32[512]{0:T(512)S(1)} %convert_element_type.257) | copy-start | bytes 6148
  228.0 65.7 %copy-start.85 = (f32[512]{0:T(512)S(1)}, f32[512]{0:T(512)}, u32[]{:S(2)}) copy-start(f32[512]{0:T(512)} %copy-done.84) | copy-start | bytes 6148
  228.0 65.7 %copy-start.24 = (bf16[2048,512]{1,0:T(8,128)(2,1)S(1)}, bf16[2048,512]{1,0:T(8,128)(2,1)}, u32[]{:S(2)}) copy-start(bf16[2048,512]{1,0:T(8,128)(2,1)} %all-gather.19.cloned.1.call-done) | copy-start | bytes 6291460
  228.0 71.4 %copy-start.83 = (f32[512]{0:T(512)S(1)}, f32[512]{0:T(512)}, u32[]{:S(2)}) copy-start(f32[512]{0:T(512)} %copy-done.82) | copy-start | bytes 6148
  228.0 223.6 %reduce-scatter.15.cloned.1.call-start = ((), (), s32[]{:S(2)}) async-start(), calls=%async_computation.19 | async-start | bytes 5242880 | tf_op jit(solution)/shard_map/reduce_scatter | solution.py:184
  346.4 105.2 %copy-start.5 = (f32[256,2048]{1,0:T(8,128)S(1)}, f32[256,2048]{1,0:T(8,128)}, u32[]{:S(2)}) copy-start(f32[256,2048]{1,0:T(8,128)} %copy-done.4) | copy-start | bytes 6291460
  346.5 162.4 %all-gather.29.cloned.1.call-start = ((), (), s32[]{:S(2)}) async-start(), calls=%async_computation.21 | async-start | bytes 9437184 | tf_op jit(solution)/shard_map/all_gather | solution.py:144
  347.2 244.0 %all-gather.35.cloned.1.call-start = ((), (), s32[]{:S(2)}) async-start(), calls=%async_computation.26 | async-start | bytes 5242880 | tf_op jit(solution)/shard_map/all_gather | solution.py:193
  457.4 214.7 %all-gather.43.cloned.1.call-start = ((), (), s32[]{:S(2)}) async-start(), calls=%async_computation.43 | async-start | bytes 5242880 | tf_op jit(solution)/shard_map/all_gather | solution.py:213
  459.8 269.0 %all-gather.31.cloned.1.call-start = ((), (), s32[]{:S(2)}) async-start(), calls=%async_computation.22 | async-start | bytes 9437184 | tf_op jit(solution)/shard_map/all_gather | solution.py:145
  460.4 351.0 %all-gather.27.cloned.1.call-start = ((), (), s32[]{:S(2)}) async-start(), calls=%async_computation.20 | async-start | bytes 5242880 | tf_op jit(solution)/shard_map/all_gather | solution.py:193
  461.1 431.0 %all-gather.41.cloned.1.call-start = ((), (), s32[]{:S(2)}) async-start(), calls=%async_computation.42 | async-start | bytes 5242880 | tf_op jit(solution)/shard_map/all_gather | solution.py:213
  461.7 507.9 %reduce-scatter.27.cloned.1.call-start = ((), (), s32[]{:S(2)}) async-start(), calls=%async_computation.31 | async-start | bytes 5242880 | tf_op jit(solution)/shard_map/reduce_scatter | solution.py:223
  762.8 286.9 %reduce-scatter.23.cloned.1.call-start = ((), (), s32[]{:S(2)}) async-start(), calls=%async_computation.28 | async-start | bytes 5242880 | tf_op jit(solution)/shard_map/reduce_scatter | solution.py:223
  926.2 203.0 %reduce-scatter.17.cloned.1.call-start = ((), (), s32[]{:S(2)}) async-start(), calls=%async_computation.23 | async-start | bytes 5242880 | tf_op jit(solution)/shard_map/reduce_scatter | solution.py:205
  942.4 266.3 %reduce-scatter.21.cloned.1.call-start = ((), (), s32[]{:S(2)}) async-start(), calls=%async_computation.27 | async-start | bytes 5242880 | tf_op jit(solution)/shard_map/reduce_scatter | solution.py:205
  958.6 91.1 %copy-start.10 = (f32[256,2048]{1,0:T(8,128)S(1)}, f32[256,2048]{1,0:T(8,128)}, u32[]{:S(2)}) copy-start(f32[256,2048]{1,0:T(8,128)} %copy-done.9) | copy-start | bytes 6291460
  958.6 91.1 %copy-start.49 = (f32[2048]{0:T(1024)S(1)}, f32[2048]{0:T(1024)}, u32[]{:S(2)}) copy-start(f32[2048]{0:T(1024)} %param.43) | copy-start | bytes 24580
  958.6 91.1 %copy-start.61 = (f32[256]{0:T(256)S(1)}, f32[256]{0:T(256)}, u32[]{:S(2)}) copy-start(f32[256]{0:T(256)} %copy-done.60) | copy-start | bytes 3076
  958.6 91.1 %copy-start.63 = (f32[256]{0:T(256)S(1)}, f32[256]{0:T(256)}, u32[]{:S(2)}) copy-start(f32[256]{0:T(256)} %copy-done.62) | copy-start | bytes 3076
  958.6 91.1 %copy-start.70 = (f32[256]{0:T(256)S(1)}, f32[256]{0:T(256)}, u32[]{:S(2)}) copy-start(f32[256]{0:T(256)} %copy-done.69) | copy-start | bytes 3076
  958.7 91.1 %copy-start.72 = (f32[256]{0:T(256)S(1)}, f32[256]{0:T(256)}, u32[]{:S(2)}) copy-start(f32[256]{0:T(256)} %copy-done.71) | copy-start | bytes 3076
  958.7 340.8 %all-gather.37.cloned.1.call-start = ((), (), s32[]{:S(2)}) async-start(), calls=%async_computation.29 | async-start | bytes 5242880 | tf_op jit(solution)/shard_map/all_gather | solution.py:227
  1218.1 234.9 %all-gather.39.cloned.1.call-start = ((), (), s32[]{:S(2)}) async-start(), calls=%async_computation.32 | async-start | bytes 5242880 | tf_op jit(solution)/shard_map/all_gather | solution.py:227
  1219.3 428.4 %reduce-scatter.39.cloned.1.call-start = ((), (), s32[]{:S(2)}) async-start(), calls=%async_computation.40 | async-start | bytes 9437184 | tf_op jit(solution)/shard_map/reduce_scatter | solution.py:320
  1249.5 401.1 %reduce-scatter.41.cloned.1.call-start = ((), (), s32[]{:S(2)}) async-start(), calls=%async_computation.41 | async-start | bytes 9437184 | tf_op jit(solution)/shard_map/reduce_scatter | solution.py:323
  1288.9 364.5 %reduce-scatter.25.cloned.1.call-start = ((), (), s32[]{:S(2)}) async-start(), calls=%async_computation.30 | async-start | bytes 5242880 | tf_op jit(solution)/shard_map/reduce_scatter | solution.py:279
  1381.7 18.8 slice-start.3
  1453.0 235.0 %reduce-scatter.29.cloned.1.call-start = ((), (), s32[]{:S(2)}) async-start(), calls=%async_computation.33 | async-start | bytes 5242880 | tf_op jit(solution)/shard_map/reduce_scatter | solution.py:279
  1609.2 123.8 %reduce-scatter.37.cloned.1.call-start = ((), (), s32[]{:S(2)}) async-start(), calls=%async_computation.39 | async-start | bytes 2359296 | tf_op jit(solution)/shard_map/reduce_scatter | solution.py:317
  1618.9 158.9 %reduce-scatter.35.cloned.1.call-start = ((), (), s32[]{:S(2)}) async-start(), calls=%async_computation.38 | async-start | bytes 2359296 | tf_op jit(solution)/shard_map/reduce_scatter | solution.py:314
  1627.7 194.4 %reduce-scatter.33.cloned.1.call-start = ((), (), s32[]{:S(2)}) async-start(), calls=%async_computation.37 | async-start | bytes 2359296 | tf_op jit(solution)/shard_map/reduce_scatter | solution.py:311
  1636.4 230.6 %reduce-scatter.31.cloned.1.call-start = ((), (), s32[]{:S(2)}) async-start(), calls=%async_computation.36 | async-start | bytes 2359296 | tf_op jit(solution)/shard_map/reduce_scatter | solution.py:308
  1646.1 264.5 %all-reduce.5.cloned.1.call-start = ((), (), s32[]{:S(2)}) async-start(), calls=%async_computation.34 | async-start | bytes 917504 | tf_op jit(solution)/shard_map/psum | solution.py:329
  1647.7 40.3 %copy-start.59 = (f32[256]{0:T(256)S(1)}, f32[256]{0:T(256)}, u32[]{:S(2)}) copy-start(f32[256]{0:T(256)} %copy-done.58) | copy-start | bytes 3076
  1647.7 40.3 %copy-start.68 = (f32[256]{0:T(256)S(1)}, f32[256]{0:T(256)}, u32[]{:S(2)}) copy-start(f32[256]{0:T(256)} %copy-done.67) | copy-start | bytes 3076
  1655.6 37.4 %copy-start.74 = (s32[256]{0:T(256)S(1)}, s32[256]{0:T(256)}, u32[]{:S(2)}) copy-start(s32[256]{0:T(256)} %copy-done.73) | copy-start | bytes 3076
  1696.3 214.4 %copy-start.17 = (f32[256,2048]{1,0:T(8,128)S(1)}, f32[256,2048]{1,0:T(8,128)}, u32[]{:S(2)}) copy-start(f32[256,2048]{1,0:T(8,128)} %copy-done.16) | copy-start | bytes 6291460
  1698.0 266.4 %all-reduce.7.cloned.1.call-start = ((), (), s32[]{:S(2)}) async-start(), calls=%async_computation.35 | async-start | bytes 917504 | tf_op jit(solution)/shard_map/psum | solution.py:328
  1910.6 55.7 %copy-start.1 = (f32[50,2048]{1,0:T(8,128)S(1)}, f32[50,2048]{1,0:T(8,128)}, u32[]{:S(2)}) copy-start(f32[50,2048]{1,0:T(8,128)} %param.29) | copy-start | bytes 1228804
  (120 other events, 847.8 us)
Sparse Core Ops, SparseCore 0:
  9.9 30.3 all-gather.20
  42.5 80.3 all-gather.32
  124.8 26.8 all-gather.22
  153.4 27.8 all-gather.18
  183.1 28.1 all-gather.24
  213.3 80.3 all-gather.16
  296.0 75.3 reduce-scatter.18
  374.4 77.2 reduce-scatter.14
  453.6 55.2 all-gather.28
  510.9 80.3 all-gather.34
  592.8 79.2 all-gather.42
  673.9 54.8 all-gather.30
  731.0 80.3 all-gather.26
  812.8 79.2 all-gather.40
  894.2 75.2 reduce-scatter.26
  972.4 77.2 reduce-scatter.22
  1051.9 77.2 reduce-scatter.16
  1131.4 77.2 reduce-scatter.20
  1218.2 81.2 all-gather.36
  1300.9 79.2 all-gather.38
  1383.7 69.7 reduce-scatter.38
  1457.3 71.3 reduce-scatter.40
  1531.0 76.7 reduce-scatter.24
  1610.6 77.2 reduce-scatter.28
  1691.2 41.7 reduce-scatter.36
  1736.5 41.2 reduce-scatter.34
  1780.8 41.1 reduce-scatter.32
  1825.7 41.2 reduce-scatter.30
  1869.9 36.8 all-reduce.4
  1910.7 53.6 all-reduce.6
